TPU v7x, 256 devices: a whole 4x4x8 slice. The times are simulated.
256 devices in a mesh: ctx: 32 (over x_lo, z, core), ep: 8 (over y, x_hi).
Axes of the slice: x: 4 (x_hi: 2, x_lo: 2; x = x_hi * 2 + x_lo), y: 4, z: 8, core: 2. Of those that a mesh axis runs over, the one named last changes fastest.
Arguments:
- queries: bfloat16 [4096, 6144], P('ctx', 'ep'), may hold values from -8 to 8
- keys: bfloat16 [4096, 1024], P('ctx', 'ep'), may hold values from -4 to 4
- values: bfloat16 [4096, 1024], P('ctx', 'ep'), may hold values from -13.5 to 13.5
- gate_weight: bfloat16 [32, 6144, 2048], P('ctx', 'ep'), may hold values from -0.078125 to 0.078125
- up_weight: bfloat16 [32, 6144, 2048], P('ctx', 'ep'), may hold values from -0.078125 to 0.078125
- down_weight: bfloat16 [32, 2048, 6144], P('ctx', None, 'ep'), may hold values from -0.125 to 0.125
- expert_ids: int32 [4096, 2], P('ctx'), may hold values from 0 to 31, as said below
- route_logits: float32 [4096, 2], P('ctx'), may hold values from -6 to 6
Outputs:
- layer_out: bfloat16 [4096, 6144], P('ctx', 'ep')
Inputs may be any that keep to these rules, and one draw needn't show every extreme that they name: `expert_ids`: the two experts of a position differ. In every sequence block of 128 positions the same 2 experts are named exactly 24 times each, one further expert is named exactly 12 times, and every other expert is named at least once and at most 12 times.
All inputs are finite; a program needn't handle non-finite values.
Results may differ from a plain program's by a relative error of at most 0.017.
Values may be sent and summed in bfloat16 or wider, within the bound.
No kernel may reach another device: no remote copies, remote signals or barrier semaphores. Data moves between devices by JAX's collectives and lax.ppermute only.
A program may use at most 64 MiB of HBM per device.

v0:
```python
import jax
import jax.numpy as jnp
from jax import lax
from jax.sharding import PartitionSpec as P

H = 48
KVH = 8
HD = 128


def expert_rows(segments):
    gate_pieces = [
        jnp.dot(segment[0], segment[1], preferred_element_type=jnp.float32) for segment in segments
    ]
    up_pieces = [
        jnp.dot(segment[0], segment[2], preferred_element_type=jnp.float32) for segment in segments
    ]
    gate_part = gate_pieces[0]
    up_part = up_pieces[0]
    gate_share, up_share = (
        lax.psum_scatter(
            gate_part.astype(jnp.bfloat16), "ep", scatter_dimension=1, tiled=True
        ).astype(jnp.float32),
        lax.psum_scatter(
            up_part.astype(jnp.bfloat16), "ep", scatter_dimension=1, tiled=True
        ).astype(jnp.float32),
    )
    hidden_share = (jax.nn.silu(gate_share) * up_share).astype(jnp.bfloat16)
    row_counts = [segment[0].shape[0] for segment in segments]
    piece_rows = lax.all_gather(hidden_share, "ep", axis=1, tiled=True)
    products = []
    offset = 0
    for segment, row_count in zip(segments, row_counts):
        weight_rows = segment[3]
        products.append(jnp.dot(piece_rows, weight_rows, preferred_element_type=jnp.float32))
        offset = offset + row_count
    produced = products[0]
    return produced.astype(jnp.bfloat16)


def on_device(queries, keys, values, gate_weight, up_weight, down_weight, expert_ids, route_logits):
    tok_rows = queries.shape[0]
    my_index = lax.axis_index("ctx")
    kv_local = keys.shape[1] // HD
    groups = H // KVH
    score_scale = HD ** (-0.5)
    query_heads = queries.reshape(tok_rows, kv_local, groups, HD)
    query_pos = my_index * tok_rows + jnp.arange(tok_rows, dtype=jnp.int32)
    row_top = jnp.full((kv_local, groups, tok_rows), -1e30, jnp.float32)
    key_piece = lax.all_gather(keys, "ctx", axis=0, tiled=True)
    value_piece = lax.all_gather(values, "ctx", axis=0, tiled=True)
    length = key_piece.shape[0]
    key_heads = key_piece.reshape(length, kv_local, HD)
    value_heads = value_piece.reshape(length, kv_local, HD)
    scores = (
        jnp.einsum("tkgd,nkd->kgtn", query_heads, key_heads, preferred_element_type=jnp.float32)
        * score_scale
    )
    allowed = query_pos[:, None] >= jnp.arange(length, dtype=jnp.int32)[None, :]
    scores = jnp.where(allowed, scores, -1e30)
    new_top = jnp.maximum(row_top, jnp.max(scores, axis=-1))
    weights = jnp.where(allowed, jnp.exp(scores - new_top[..., None]), 0.0)
    row_total = jnp.sum(weights, axis=-1)
    running = jnp.einsum(
        "kgtn,nkd->kgtd",
        weights.astype(jnp.bfloat16),
        value_heads,
        preferred_element_type=jnp.float32,
    )
    row_top, row_total, running = (new_top, row_total, running)
    head_out = running / row_total[..., None]
    attended = (
        head_out.transpose(2, 0, 1, 3)
        .reshape(tok_rows, kv_local * groups * HD)
        .astype(jnp.bfloat16)
    )
    experts = lax.axis_size("ctx")
    features = attended.shape[1]
    hot_cap = 6 * tok_rows // experts
    flat_ids = expert_ids.reshape(-1)
    expert_range = jnp.arange(experts, dtype=jnp.int32)
    hit_table = (flat_ids[:, None] == expert_range[None, :]).astype(jnp.int32)
    slot_of = jnp.sum((jnp.cumsum(hit_table, axis=0) - 1) * hit_table, axis=1)
    own_gate = gate_weight[0]
    own_up = up_weight[0]
    own_down = down_weight[0]
    target = flat_ids * hot_cap + slot_of
    slot_total = experts * hot_cap
    placer = (jnp.arange(slot_total, dtype=jnp.int32)[:, None] == target[None, :]).astype(
        jnp.bfloat16
    )
    placer = jnp.sum(placer.reshape(slot_total, tok_rows, 2), axis=2)
    placed = jnp.dot(placer, attended, preferred_element_type=jnp.float32).astype(jnp.bfloat16)
    outgoing = placed.reshape(experts, hot_cap, features)
    arrived = lax.all_to_all(outgoing, "ctx", split_axis=0, concat_axis=0, tiled=True)
    segments = [(arrived.reshape(experts * hot_cap, features), own_gate, own_up, own_down)]
    produced = expert_rows(segments)
    cold_answer = produced.reshape(experts, hot_cap, features)
    came_back = lax.all_to_all(cold_answer, "ctx", split_axis=0, concat_axis=0, tiled=True)
    answer_table = came_back.reshape(experts * hot_cap, features)
    picked = jnp.take(answer_table, target, axis=0).reshape(tok_rows, 2, features)
    route_share = jax.nn.softmax(route_logits, axis=-1)
    mixture = jnp.sum(picked.astype(jnp.float32) * route_share[:, :, None], axis=1)
    return (attended.astype(jnp.float32) + mixture).astype(jnp.bfloat16)


def solution(mesh):
    in_specs = (
        P("ctx", "ep"),
        P("ctx", "ep"),
        P("ctx", "ep"),
        P("ctx", "ep", None),
        P("ctx", "ep", None),
        P("ctx", None, "ep"),
        P("ctx", None),
        P("ctx", None),
    )
    out_specs = P("ctx", "ep")
    return jax.shard_map(
        on_device, mesh=mesh, in_specs=in_specs, out_specs=out_specs, check_vma=False
    )
```

profile of v0, /device:TPU:32, one launch (start us, length us, event | category | flops | bytes accessed | tf_op | source)
XLA Modules:
  0.0 491.0 jit_solution(1740220423678054590)
XLA Ops:
  6.5 0.7 all-gather.4.cloned.1.call-update
  7.3 0.0 all-gather.6.cloned.1.call-start
  7.3 1.6 copy.39
  9.0 0.0 all-gather.6.cloned.1.call-update
  9.0 0.0 reduce-scatter.3.cloned.1.call-start
  9.0 0.8 copy.42
  9.8 0.1 eq.40
  10.0 0.1 reshape.138
  10.1 1.1 iota_compare_fusion
  11.2 0.6 reduce-window.6
  11.8 0.2 slice_reduce_fusion
  12.1 0.1 fusion.35
  12.2 0.1 reduce_sum.54
  12.3 0.1 copy.45
  12.4 0.4 copy-done.4
  12.7 1.3 compare_and_fusion
  14.0 1.1 copy.37
  15.1 0.1 fusion.33
  15.2 59.2 %all-gather.4.cloned.1.call-done = bf16[4096,128]{1,0:T(8,128)(2,1)} async-done(((bf16[128,128]{1,0:T(8,128)(2,1)}), bf16[4096,128]{1,0:T(8,128)(2,1)}) %all-gather.4.cloned.1.call-update) | async-done | bytes 1048592 | tf_op jit(solution)/shard_map/all_gather | solution.py:50
  74.4 3.4 fusion
  77.8 4.5 copy-done.1
  82.4 3.1 fusion.1
  85.5 53.3 %all-gather.6.cloned.1.call-done = bf16[4096,128]{0,1:T(8,128)(2,1)} async-done(((bf16[128,128]{0,1:T(8,128)(2,1)}), bf16[4096,128]{0,1:T(8,128)(2,1)}) %all-gather.6.cloned.1.call-update) | async-done | bytes 1048592 | tf_op jit(solution)/shard_map/all_gather | solution.py:51
  138.8 8.1 %fusion.22 = bf16[6,128,128]{1,2,0:T(8,128)(2,1)S(1)} fusion(f32[4096,128,6]{1,0,2:T(8,128)} %copy-done.1, f32[6,128]{1,0:T(8,128)S(1)} %broadcast_maximum_fusion, pred[128,4096]{0,1:T(8,128)(4,1)} %iota_compare_fusion, bf16[4096,128]{0,1:T(8,128)(2,1)} %all-gather.6.cloned.1.call-done, f32[6,128]{1,0:T(8,128)S(1)} %fusion.1), kind=kOutput, calls=%fused_computation.22 | convolution fusion | flops 821231616 | bytes 14358528 | tf_op jit(solution)/shard_map/kgtn,nkd->kgtd/dot_general | solution.py:64
  146.9 0.5 convolution_convert_fusion.2
  147.4 36.9 %all_to_all.10 = bf16[32,24,768]{2,1,0:T(8,128)(2,1)S(1)} all-to-all(bf16[32,24,768]{2,1,0:T(8,128)(2,1)S(1)} %bitcast.82), channel_id=1, replica_groups=mesh['ctx'=32,'ep'=8] {'ctx'}, dimensions={0} | all-to-all | bytes 2359296 | tf_op jit(solution)/shard_map/all_to_all | solution.py:95
  184.3 1.0 copy-done.3
  185.4 4.0 convolution_convert_fusion.1
  189.4 0.0 reduce-scatter.5.cloned.1.call-start
  189.4 6.6 %convolution_convert_fusion = bf16[768,2048]{1,0:T(8,128)(2,1)} fusion(bf16[768,768]{1,0:T(8,128)(2,1)} %bitcast.85, bf16[1,768,2048]{2,1,0:T(8,128)(2,1)} %param.12), kind=kOutput, calls=%fused_computation.9 | convolution fusion | flops 2417491968 | bytes 7471104 | tf_op jit(solution)/shard_map/dot_general | solution.py:16
  196.0 0.0 reduce-scatter.5.cloned.1.call-update
  196.0 0.2 all-gather.8.cloned.1.call-start
  196.3 75.8 %reduce-scatter.3.cloned.1.call-done = bf16[768,256]{1,0:T(8,128)(2,1)} async-done(((bf16[768,2048]{1,0:T(8,128)(2,1)}), bf16[768,256]{1,0:T(8,128)(2,1)}) %reduce-scatter.3.cloned.1.call-update) | async-done | bytes 393232 | tf_op jit(solution)/shard_map/reduce_scatter | solution.py:21
  272.0 88.2 %reduce-scatter.5.cloned.1.call-done = bf16[768,256]{1,0:T(8,128)(2,1)} async-done(((bf16[768,2048]{1,0:T(8,128)(2,1)}), bf16[768,256]{1,0:T(8,128)(2,1)}) %reduce-scatter.5.cloned.1.call-update) | async-done | bytes 393232 | tf_op jit(solution)/shard_map/reduce_scatter | solution.py:24
  360.3 2.1 fusion.31
  362.4 67.5 %all-gather.8.cloned.1.call-done = bf16[768,2048]{1,0:T(8,128)(2,1)} async-done(((bf16[768,256]{1,0:T(8,128)(2,1)}), bf16[768,2048]{1,0:T(8,128)(2,1)}) %all-gather.8.cloned.1.call-update) | async-done | bytes 3145744 | tf_op jit(solution)/shard_map/all_gather | solution.py:30
  429.9 6.5 %fusion.11 = bf16[768,768]{1,0:T(8,128)(2,1)} fusion(bf16[768,2048]{1,0:T(8,128)(2,1)} %all-gather.8.cloned.1.call-done, bf16[1,2048,768]{2,1,0:T(8,128)(2,1)} %param.13), kind=kOutput, calls=%fused_computation.16 | convolution fusion | flops 2416508928 | bytes 7471104 | tf_op jit(solution)/shard_map/dot_general | solution.py:35
  436.4 7.7 %all-to-all-start.1 = ((bf16[32,24,768]{2,1,0:T(8,128)(2,1)}), bf16[32,24,768]{2,1,0:T(8,128)(2,1)}, u32[]{:S(2)}, u32[]{:S(2)}) async-start(bf16[32,24,768]{2,1,0:T(8,128)(2,1)} %bitcast.83), calls=%async_computation.3 | async-start | bytes 2359296 | tf_op jit(solution)/shard_map/all_to_all | solution.py:99
  444.1 0.1 copy.47
  444.2 0.1 mul.66
  444.4 0.1 copy.46
  444.6 0.7 copy.48
  445.3 0.8 copy.41
  446.2 29.8 %all-to-all-done.1 = bf16[32,24,768]{2,1,0:T(8,128)(2,1)} async-done(((bf16[32,24,768]{2,1,0:T(8,128)(2,1)}), bf16[32,24,768]{2,1,0:T(8,128)(2,1)}, u32[]{:S(2)}, u32[]{:S(2)}) %all-to-all-start.1) | async-done | bytes 1179680 | tf_op jit(solution)/shard_map/all_to_all | solution.py:99
  475.9 3.6 gather_fusion
  479.5 1.1 gather.7
  480.7 2.1 multiply_reduce_fusion
  482.8 1.7 add_convert_fusion
  (29 shorter events, 0.2 us)
Async XLA Ops:
  6.5 178.8 %copy-start = (bf16[1,768,2048]{2,1,0:T(8,128)(2,1)S(1)}, bf16[1,768,2048]{2,1,0:T(8,128)(2,1)}, u32[]{:S(2)}) copy-start(bf16[1,768,2048]{2,1,0:T(8,128)(2,1)} %param.11) | copy-start | bytes 9437188
  6.5 67.9 %all-gather.4.cloned.1.call-start = ((), (), s32[]{:S(2)}) async-start(), calls=%async_computation.4 | async-start | bytes 1081344 | tf_op jit(solution)/shard_map/all_gather | solution.py:50
  7.3 131.5 %all-gather.6.cloned.1.call-start = ((), (), s32[]{:S(2)}) async-start(), calls=%async_computation.5 | async-start | bytes 1081344 | tf_op jit(solution)/shard_map/all_gather | solution.py:51
  9.0 263.1 %reduce-scatter.3.cloned.1.call-start = ((), (), s32[]{:S(2)}) async-start(), calls=%async_computation.6 | async-start | bytes 3538944 | tf_op jit(solution)/shard_map/reduce_scatter | solution.py:21
  12.2 0.6 copy-start.4
  74.4 7.9 %copy-start.2 = (pred[128,4096]{0,1:T(8,128)(4,1)S(1)}, pred[128,4096]{0,1:T(8,128)(4,1)}, u32[]{:S(2)}) copy-start(pred[128,4096]{0,1:T(8,128)(4,1)} %iota_compare_fusion) | copy-start | bytes 1572868
  77.8 4.6 copy-start.1
  184.3 1.0 copy-start.3
  189.4 170.9 %reduce-scatter.5.cloned.1.call-start = ((), (), s32[]{:S(2)}) async-start(), calls=%async_computation.7 | async-start | bytes 3538944 | tf_op jit(solution)/shard_map/reduce_scatter | solution.py:24
  196.0 233.9 %all-gather.8.cloned.1.call-start = ((), (), s32[]{:S(2)}) async-start(), calls=%async_computation.8 | async-start | bytes 3538944 | tf_op jit(solution)/shard_map/all_gather | solution.py:30
  362.4 81.7 %copy-start.6 = (s32[128,2]{0,1:T(2,128)S(1)}, s32[128,2]{0,1:T(2,128)}, u32[]{:S(2)}) copy-start(s32[128,2]{0,1:T(2,128)} %param.14) | copy-start | bytes 3076
  362.4 82.0 %copy-start.8 = (pred[128,2]{0,1:T(4,128)(4,1)S(1)}, pred[128,2]{0,1:T(4,128)(4,1)}, u32[]{:S(2)}) copy-start(pred[128,2]{0,1:T(4,128)(4,1)} %get-tuple-element.5) | copy-start | bytes 772
  362.4 82.1 %copy-start.7 = (f32[128,2]{0,1:T(2,128)S(1)}, f32[128,2]{0,1:T(2,128)}, u32[]{:S(2)}) copy-start(f32[128,2]{0,1:T(2,128)} %param.15) | copy-start | bytes 3076
  362.4 82.9 %copy-start.5 = (s32[256]{0:T(256)S(1)}, s32[256]{0:T(256)}, u32[]{:S(2)}) copy-start(s32[256]{0:T(256)} %copy-done.4) | copy-start | bytes 3076
  436.4 39.5 %all-to-all-start.1 = ((bf16[32,24,768]{2,1,0:T(8,128)(2,1)}), bf16[32,24,768]{2,1,0:T(8,128)(2,1)}, u32[]{:S(2)}, u32[]{:S(2)}) async-start(bf16[32,24,768]{2,1,0:T(8,128)(2,1)} %bitcast.83), calls=%async_computation.3 | async-start | bytes 2359296 | tf_op jit(solution)/shard_map/all_to_all | solution.py:99
Sparse Core Ops, SparseCore 0:
  9.2 65.2 all-gather.3
  76.2 62.5 all-gather.5
  189.5 82.4 reduce-scatter.2
  276.0 84.1 reduce-scatter.4
  362.6 67.3 all-gather.7
where the time goes:
time: 491 us
  waiting for transfers between devices  375 us (76%)
  blocking collectives  36.9 us (8%)
  matrix products  29 us (6%)
  local copies, waits for them, and re-layouts  16.9 us (3%)
  between operations  13.3 us (3%)
  other arithmetic  12.2 us (2%)
  starting transfers between devices  8.04 us (2%)
    reduce_scatter x1, waiting for transfers between devices, expert_rows(): lax.psum_scatter(up_part.astype(jnp.bfloat16), 'ep', scatter_dimension=1,...  88.2 us
    reduce_scatter x1, waiting for transfers between devices, expert_rows(): lax.psum_scatter(gate_part.astype(jnp.bfloat16), 'ep', scatter_dimension=...  75.8 us
    all_gather x1, waiting for transfers between devices, expert_rows(): piece_rows = lax.all_gather(hidden_share, 'ep', axis=1, tiled=True)  67.5 us
    all_gather x1, waiting for transfers between devices, on_device(): key_piece = lax.all_gather(keys, 'ctx', axis=0, tiled=True)  59.2 us
    all_gather x1, waiting for transfers between devices, on_device(): value_piece = lax.all_gather(values, 'ctx', axis=0, tiled=True)  53.3 us
    all_to_all x1, blocking collectives, on_device(): lax.all_to_all(outgoing, 'ctx', split_axis=0, concat_axis=0, tiled=True)  36.9 us
    all_to_all x1, waiting for transfers between devices, on_device(): lax.all_to_all(cold_answer, 'ctx', split_axis=0, concat_axis=0, tiled=True)  29.8 us
  transfers between devices with their start and end apart: 6, of which 6 were waited for; matrix products, arithmetic and copies ran while one was open for 5% of the time, Pallas kernels for 0%

commit v1 on v0

--- a/solution.py
+++ b/solution.py
@@ -47,7 +47,9 @@
     query_heads = queries.reshape(tok_rows, kv_local, groups, HD)
     query_pos = my_index * tok_rows + jnp.arange(tok_rows, dtype=jnp.int32)
     row_top = jnp.full((kv_local, groups, tok_rows), -1e30, jnp.float32)
-    key_piece = lax.all_gather(keys, "ctx", axis=0, tiled=True)
+    key_piece = jnp.concatenate(
+        lax.all_to_all(jnp.stack([keys] * lax.axis_size("ctx")), "ctx", 0, 0), axis=0
+    )
     value_piece = lax.all_gather(values, "ctx", axis=0, tiled=True)
     length = key_piece.shape[0]
     key_heads = key_piece.reshape(length, kv_local, HD)

time: 491 us -> 439 us (0.89)
  waiting for transfers between devices: 375 us -> 313 us
  starting transfers between devices: 8.04 us -> 17.7 us
    all_gather x1 -> x0, waiting for transfers between devices: 59.2 us -> none  [on_device(): key_piece = lax.all_gather(keys, 'ctx', axis=0, tiled=True)]
    all_gather x1, waiting for transfers between devices: 53.3 us -> 27.3 us  [on_device(): value_piece = lax.all_gather(values, 'ctx', axis=0, tiled=True)]
    all_to_all x0 -> x1, waiting for transfers between devices: none -> 24.7 us  [on_device(): lax.all_to_all(jnp.stack([keys] * lax.axis_size('ctx')), 'ctx', 0, 0)]
    all_to_all x0 -> x1, starting transfers between devices: none -> 9.71 us  [on_device(): lax.all_to_all(jnp.stack([keys] * lax.axis_size('ctx')), 'ctx', 0, 0)]
where the time goes in v1:
time: 439 us; the launch traced here: 438 us
  waiting for transfers between devices  313 us (71%)
  blocking collectives  37.2 us (8%)
  matrix products  29.1 us (7%)
  starting transfers between devices  17.7 us (4%)
  local copies, waits for them, and re-layouts  16.8 us (4%)
  between operations  13.3 us (3%)
  other arithmetic  11.6 us (3%)
    reduce_scatter x1, waiting for transfers between devices, expert_rows(): lax.psum_scatter(up_part.astype(jnp.bfloat16), 'ep', scatter_dimension=1,...  88.4 us
    reduce_scatter x1, waiting for transfers between devices, expert_rows(): lax.psum_scatter(gate_part.astype(jnp.bfloat16), 'ep', scatter_dimension=...  74.9 us
    all_gather x1, waiting for transfers between devices, expert_rows(): piece_rows = lax.all_gather(hidden_share, 'ep', axis=1, tiled=True)  67.5 us
    all_to_all x1, blocking collectives, on_device(): lax.all_to_all(outgoing, 'ctx', split_axis=0, concat_axis=0, tiled=True)  37.2 us
    all_to_all x1, waiting for transfers between devices, on_device(): lax.all_to_all(cold_answer, 'ctx', split_axis=0, concat_axis=0, tiled=True)  29.8 us
    all_gather x1, waiting for transfers between devices, on_device(): value_piece = lax.all_gather(values, 'ctx', axis=0, tiled=True)  27.3 us
    all_to_all x1, waiting for transfers between devices, on_device(): lax.all_to_all(jnp.stack([keys] * lax.axis_size('ctx')), 'ctx', 0, 0)  24.7 us
    all_to_all x1, starting transfers between devices, on_device(): lax.all_to_all(jnp.stack([keys] * lax.axis_size('ctx')), 'ctx', 0, 0)  9.71 us
  transfers between devices with their start and end apart: 6, of which 6 were waited for; matrix products, arithmetic and copies ran while one was open for 5% of the time, Pallas kernels for 0%

profile of v1, /device:TPU:32, one launch (start us, length us, event | category | flops | bytes accessed | tf_op | source)
XLA Modules:
  0.0 438.3 jit_solution(3789201431100860066)
XLA Ops:
  6.5 2.2 stack.2
  8.7 9.7 %all-to-all-start = ((bf16[32,128,128]{2,1,0:T(8,128)(2,1)}), bf16[32,128,128]{2,1,0:T(8,128)(2,1)}, u32[]{:S(2)}, u32[]{:S(2)}) async-start(bf16[32,128,128]{2,1,0:T(8,128)(2,1)} %stack.2), calls=%async_computation | async-start | bytes 2097152 | tf_op jit(solution)/shard_map/all_to_all | solution.py:51
  18.4 0.0 all-gather.3.cloned.1.call-start
  18.5 0.7 copy.39
  19.2 0.0 all-gather.3.cloned.1.call-update
  19.2 0.0 reduce-scatter.3.cloned.1.call-start
  19.3 0.1 copy.42
  19.4 0.1 eq.40
  19.6 0.1 reshape.142
  19.7 0.6 reduce-window.6
  20.3 0.2 slice_reduce_fusion
  20.5 0.1 fusion.33
  20.6 0.1 reduce_sum.54
  20.8 0.1 copy.45
  20.9 1.2 iota_compare_fusion
  22.0 0.6 compare_and_fusion
  22.6 0.8 copy.37
  23.4 0.1 fusion.31
  23.5 24.7 %all-to-all-done = bf16[32,128,128]{2,1,0:T(8,128)(2,1)} async-done(((bf16[32,128,128]{2,1,0:T(8,128)(2,1)}), bf16[32,128,128]{2,1,0:T(8,128)(2,1)}, u32[]{:S(2)}, u32[]{:S(2)}) %all-to-all-start) | async-done | bytes 1048608 | tf_op jit(solution)/shard_map/all_to_all | solution.py:51
  48.2 3.5 fusion
  51.7 4.5 %copy-done.1 = f32[4096,128,6]{1,0,2:T(8,128)} copy-done((f32[4096,128,6]{1,0,2:T(8,128)}, f32[4096,128,6]{1,0,2:T(8,128)S(1)}, u32[]{:S(2)}) %copy-start.1) | copy-done | bytes 12582936
  56.2 3.1 fusion.1
  59.3 27.3 %all-gather.3.cloned.1.call-done = bf16[4096,128]{0,1:T(8,128)(2,1)} async-done(((bf16[128,128]{0,1:T(8,128)(2,1)}), bf16[4096,128]{0,1:T(8,128)(2,1)}) %all-gather.3.cloned.1.call-update) | async-done | bytes 1048592 | tf_op jit(solution)/shard_map/all_gather | solution.py:53
  86.6 8.1 %fusion.20 = bf16[6,128,128]{1,2,0:T(8,128)(2,1)S(1)} fusion(f32[4096,128,6]{1,0,2:T(8,128)} %copy-done.1, f32[6,128]{1,0:T(8,128)S(1)} %broadcast_maximum_fusion, pred[128,4096]{0,1:T(8,128)(4,1)} %iota_compare_fusion, bf16[4096,128]{0,1:T(8,128)(2,1)} %all-gather.3.cloned.1.call-done, f32[6,128]{1,0:T(8,128)S(1)} %fusion.1), kind=kOutput, calls=%fused_computation.20 | convolution fusion | flops 821231616 | bytes 14358528 | tf_op jit(solution)/shard_map/kgtn,nkd->kgtd/dot_general | solution.py:66
  94.7 0.5 convolution_convert_fusion.2
  95.2 37.2 %all_to_all.15 = bf16[32,24,768]{2,1,0:T(8,128)(2,1)S(1)} all-to-all(bf16[32,24,768]{2,1,0:T(8,128)(2,1)S(1)} %bitcast.81), channel_id=1, replica_groups=mesh['ctx'=32,'ep'=8] {'ctx'}, dimensions={0} | all-to-all | bytes 2359296 | tf_op jit(solution)/shard_map/all_to_all | solution.py:97
  132.3 1.0 copy-done.3
  133.4 4.0 convolution_convert_fusion.1
  137.4 0.0 reduce-scatter.3.cloned.1.call-update
  137.4 0.0 reduce-scatter.5.cloned.1.call-start
  137.5 6.6 %convolution_convert_fusion = bf16[768,2048]{1,0:T(8,128)(2,1)} fusion(bf16[768,768]{1,0:T(8,128)(2,1)} %bitcast.84, bf16[1,768,2048]{2,1,0:T(8,128)(2,1)} %param.12), kind=kOutput, calls=%fused_computation.9 | convolution fusion | flops 2417491968 | bytes 7471104 | tf_op jit(solution)/shard_map/dot_general | solution.py:16
  144.0 0.2 all-gather.5.cloned.1.call-start
  144.3 74.9 %reduce-scatter.3.cloned.1.call-done = bf16[768,256]{1,0:T(8,128)(2,1)} async-done(((bf16[768,2048]{1,0:T(8,128)(2,1)}), bf16[768,256]{1,0:T(8,128)(2,1)}) %reduce-scatter.3.cloned.1.call-update) | async-done | bytes 393232 | tf_op jit(solution)/shard_map/reduce_scatter | solution.py:21
  219.2 88.4 %reduce-scatter.5.cloned.1.call-done = bf16[768,256]{1,0:T(8,128)(2,1)} async-done(((bf16[768,2048]{1,0:T(8,128)(2,1)}), bf16[768,256]{1,0:T(8,128)(2,1)}) %reduce-scatter.5.cloned.1.call-update) | async-done | bytes 393232 | tf_op jit(solution)/shard_map/reduce_scatter | solution.py:24
  307.6 2.1 fusion.29
  309.8 67.5 %all-gather.5.cloned.1.call-done = bf16[768,2048]{1,0:T(8,128)(2,1)} async-done(((bf16[768,256]{1,0:T(8,128)(2,1)}), bf16[768,2048]{1,0:T(8,128)(2,1)}) %all-gather.5.cloned.1.call-update) | async-done | bytes 3145744 | tf_op jit(solution)/shard_map/all_gather | solution.py:30
  377.3 6.5 %fusion.11 = bf16[768,768]{1,0:T(8,128)(2,1)} fusion(bf16[768,2048]{1,0:T(8,128)(2,1)} %all-gather.5.cloned.1.call-done, bf16[1,2048,768]{2,1,0:T(8,128)(2,1)} %param.13), kind=kOutput, calls=%fused_computation.16 | convolution fusion | flops 2416508928 | bytes 7471104 | tf_op jit(solution)/shard_map/dot_general | solution.py:35
  383.7 7.7 %all-to-all-start.2 = ((bf16[32,24,768]{2,1,0:T(8,128)(2,1)}), bf16[32,24,768]{2,1,0:T(8,128)(2,1)}, u32[]{:S(2)}, u32[]{:S(2)}) async-start(bf16[32,24,768]{2,1,0:T(8,128)(2,1)} %bitcast.82), calls=%async_computation.4 | async-start | bytes 2359296 | tf_op jit(solution)/shard_map/all_to_all | solution.py:101
  391.5 0.1 copy.47
  391.6 0.1 mul.66
  391.7 0.1 copy.46
  391.9 0.7 copy.48
  392.7 0.8 copy.41
  393.5 29.8 %all-to-all-done.2 = bf16[32,24,768]{2,1,0:T(8,128)(2,1)} async-done(((bf16[32,24,768]{2,1,0:T(8,128)(2,1)}), bf16[32,24,768]{2,1,0:T(8,128)(2,1)}, u32[]{:S(2)}, u32[]{:S(2)}) %all-to-all-start.2) | async-done | bytes 1179680 | tf_op jit(solution)/shard_map/all_to_all | solution.py:101
  423.3 3.6 gather_fusion
  426.9 1.1 gather.7
  428.0 2.1 multiply_reduce_fusion
  430.1 1.7 add_convert_fusion
  (33 shorter events, 0.2 us)
Async XLA Ops:
  6.5 126.8 %copy-start = (bf16[1,768,2048]{2,1,0:T(8,128)(2,1)S(1)}, bf16[1,768,2048]{2,1,0:T(8,128)(2,1)}, u32[]{:S(2)}) copy-start(bf16[1,768,2048]{2,1,0:T(8,128)(2,1)} %param.11) | copy-start | bytes 9437188
  6.5 12.0 %copy-start.5 = (bf16[128,128]{1,0:T(8,128)(2,1)S(1)}, bf16[128,128]{1,0:T(8,128)(2,1)}, u32[]{:S(2)}) copy-start(bf16[128,128]{1,0:T(8,128)(2,1)} %param.10) | copy-start | bytes 98308
  6.5 12.7 %copy-start.8 = (s32[128,2]{0,1:T(2,128)S(1)}, s32[128,2]{0,1:T(2,128)}, u32[]{:S(2)}) copy-start(s32[128,2]{0,1:T(2,128)} %param.14) | copy-start | bytes 3076
  6.5 16.0 %copy-start.4 = (bf16[128,768]{1,0:T(8,128)(2,1)S(1)}, bf16[128,768]{1,0:T(8,128)(2,1)}, u32[]{:S(2)}) copy-start(bf16[128,768]{1,0:T(8,128)(2,1)} %param.8) | copy-start | bytes 589828
  8.7 39.4 %all-to-all-start = ((bf16[32,128,128]{2,1,0:T(8,128)(2,1)}), bf16[32,128,128]{2,1,0:T(8,128)(2,1)}, u32[]{:S(2)}, u32[]{:S(2)}) async-start(bf16[32,128,128]{2,1,0:T(8,128)(2,1)} %stack.2), calls=%async_computation | async-start | bytes 2097152 | tf_op jit(solution)/shard_map/all_to_all | solution.py:51
  18.4 68.1 %all-gather.3.cloned.1.call-start = ((), (), s32[]{:S(2)}) async-start(), calls=%async_computation.5 | async-start | bytes 1081344 | tf_op jit(solution)/shard_map/all_gather | solution.py:53
  19.2 200.0 %reduce-scatter.3.cloned.1.call-start = ((), (), s32[]{:S(2)}) async-start(), calls=%async_computation.6 | async-start | bytes 3538944 | tf_op jit(solution)/shard_map/reduce_scatter | solution.py:21
  20.6 2.8 copy-start.6
  48.2 8.0 %copy-start.2 = (pred[128,4096]{0,1:T(8,128)(4,1)S(1)}, pred[128,4096]{0,1:T(8,128)(4,1)}, u32[]{:S(2)}) copy-start(pred[128,4096]{0,1:T(8,128)(4,1)} %iota_compare_fusion) | copy-start | bytes 1572868
  51.6 4.6 %copy-start.1 = (f32[4096,128,6]{1,0,2:T(8,128)}, f32[4096,128,6]{1,0,2:T(8,128)S(1)}, u32[]{:S(2)}) copy-start(f32[4096,128,6]{1,0,2:T(8,128)S(1)} %get-tuple-element.8) | copy-start | bytes 37748740
  132.3 1.0 copy-start.3
  137.4 170.2 %reduce-scatter.5.cloned.1.call-start = ((), (), s32[]{:S(2)}) async-start(), calls=%async_computation.7 | async-start | bytes 3538944 | tf_op jit(solution)/shard_map/reduce_scatter | solution.py:24
  144.0 233.2 %all-gather.5.cloned.1.call-start = ((), (), s32[]{:S(2)}) async-start(), calls=%async_computation.8 | async-start | bytes 3538944 | tf_op jit(solution)/shard_map/all_gather | solution.py:30
  309.7 82.0 %copy-start.10 = (pred[128,2]{0,1:T(4,128)(4,1)S(1)}, pred[128,2]{0,1:T(4,128)(4,1)}, u32[]{:S(2)}) copy-start(pred[128,2]{0,1:T(4,128)(4,1)} %get-tuple-element.5) | copy-start | bytes 772
  309.7 82.1 %copy-start.9 = (f32[128,2]{0,1:T(2,128)S(1)}, f32[128,2]{0,1:T(2,128)}, u32[]{:S(2)}) copy-start(f32[128,2]{0,1:T(2,128)} %param.15) | copy-start | bytes 3076
  309.7 82.9 %copy-start.7 = (s32[256]{0:T(256)S(1)}, s32[256]{0:T(256)}, u32[]{:S(2)}) copy-start(s32[256]{0:T(256)} %copy-done.6) | copy-start | bytes 3076
  383.7 39.5 %all-to-all-start.2 = ((bf16[32,24,768]{2,1,0:T(8,128)(2,1)}), bf16[32,24,768]{2,1,0:T(8,128)(2,1)}, u32[]{:S(2)}, u32[]{:S(2)}) async-start(bf16[32,24,768]{2,1,0:T(8,128)(2,1)} %bitcast.82), calls=%async_computation.4 | async-start | bytes 2359296 | tf_op jit(solution)/shard_map/all_to_all | solution.py:101
Sparse Core Ops, SparseCore 0:
  21.0 65.5 all-gather.2
  137.5 81.6 reduce-scatter.2
  223.3 84.1 reduce-scatter.4
  309.9 67.3 all-gather.4
